TPU v7x, 256 devices: a whole 4x4x8 slice. The times are simulated.
256 devices in a mesh: ja: 16 (over z, core), ka: 16 (over x, y).
Axes of the slice: x: 4, y: 4, z: 8, core: 2. Of those that a mesh axis runs over, the one named last changes fastest.
Arguments:
- tensor: float32 [64, 1024, 1024], P('ka', 'ja'), may hold values from -6 to 6
- factor_one: float32 [1024, 256], replicated, may hold values from -0.1875 to 0.1875
- factor_two: bfloat16 [1024, 256], P('ja'), may hold values from -0.1875 to 0.1875
Outputs:
- gram_one: float32 [1024, 1024], P(('ja', 'ka'))
- gram_two: float32 [1024, 1024], P(('ja', 'ka'))
- reduced: float32 [64, 256, 256], P('ka', 'ja')
All inputs are finite; a program needn't handle non-finite values.
Results may differ from a plain program's by a relative error of at most 0.0029.
Values may be sent and summed in bfloat16 or wider, within the bound.
A program may use at most 64 MiB of HBM per device.

v0:
```python
import math

import jax
import jax.numpy as jnp
from jax import lax
from jax.sharding import PartitionSpec as P


def split_up(array, dim, devices):
    dims = array.shape
    blocks = array.reshape(*dims[:dim], devices, dims[dim] // devices, *dims[dim + 1 :])
    return jnp.moveaxis(blocks, dim, 0)


def sum_at_owner(array, axis, dim):
    blocks = split_up(array, dim, lax.axis_size(axis))
    arrived = lax.all_to_all(blocks, axis, split_axis=0, concat_axis=0, tiled=True)
    return arrived.sum(axis=0)


def copy_for_each(array, axis):
    devices = lax.axis_size(axis)
    return lax.all_to_all(
        jnp.broadcast_to(array[None], (devices, *array.shape)), axis, 0, 0, tiled=True
    )


def laid_out(blocks, dim):
    blocks = jnp.moveaxis(blocks, 0, dim)
    dims = blocks.shape
    return blocks.reshape(*dims[:dim], dims[dim] * dims[dim + 1], *dims[dim + 2 :])


def gathered_copies(array, axis, dim):
    blocks = copy_for_each(array, axis)
    return laid_out(blocks, dim)


def shards(tensor, factor_one, factor_two):
    slices, owned, width = tensor.shape
    count_ja = lax.axis_size("ja")
    count_ka = lax.axis_size("ka")
    flat = tensor.reshape(slices * owned, width)
    halfway = lax.psum_scatter(
        jnp.dot(flat.T, flat, precision=lax.Precision.HIGHEST, preferred_element_type=jnp.float32),
        "ja",
        scatter_dimension=0,
        tiled=True,
    )
    summed = sum_at_owner(halfway, "ka", 0)
    gram_one = summed * (1.0 / math.sqrt(owned * count_ja * slices * count_ka))
    rank_one = factor_one.shape[1]
    core = jnp.dot(
        flat, factor_one, precision=lax.Precision.HIGHEST, preferred_element_type=jnp.float32
    )
    core = core.astype(jnp.bfloat16).reshape(slices, owned, rank_one)
    norm_two = 1.0 / math.sqrt(slices * count_ka * rank_one)
    blocks = jnp.einsum(
        "kjr,klr->jl", core, gathered_copies(core, "ja", 1), preferred_element_type=jnp.float32
    )
    gram_two = sum_at_owner(blocks, "ka", 0)
    partial_value = jnp.einsum("kjr,js->ksr", core, factor_two, preferred_element_type=jnp.float32)
    reduced = sum_at_owner(partial_value, "ja", 1)
    return (gram_one, gram_two * norm_two, reduced)


def solution(mesh):
    in_specs = (P("ka", "ja", None), P(), P("ja", None))
    out_specs = (P(("ja", "ka"), None), P(("ja", "ka"), None), P("ka", "ja", None))
    return jax.shard_map(shards, mesh=mesh, in_specs=in_specs, out_specs=out_specs, check_vma=False)
```

profile of v0, /device:TPU:1, one launch (start us, length us, event | category | flops | bytes accessed | tf_op | source)
XLA Modules:
  0.0 155.0 jit_solution(5541640882035176645)
XLA Ops:
  7.2 0.0 copy-start
  7.2 0.0 reduce-scatter.2.cloned.1.call-start
  7.2 1.2 copy-done
  8.4 5.0 %convolution_bitcast_fusion = f32[1024,1024]{1,0:T(8,128)} fusion(f32[4,64,1024]{2,1,0:T(8,128)S(1)} %copy-done), kind=kOutput, calls=%fused_computation | convolution fusion | flops 3221225472 | bytes 5242880 | tf_op jit(solution)/shard_map/dot_general | solution.py:45
  13.4 0.0 copy-start.1
  13.4 0.0 reduce-scatter.2.cloned.1.call-update
  13.4 1.2 copy-done.1
  14.6 1.0 convolution_convert_fusion
  15.7 1.6 %broadcast_in_dim.2 = bf16[16,4,64,256]{3,2,1,0:T(8,128)(2,1)} broadcast(bf16[4,64,256]{2,1,0:T(8,128)(2,1)S(1)} %bitcast.34), dimensions={1,2,3} | broadcast | bytes 2228224 | tf_op jit(solution)/shard_map/broadcast_in_dim | solution.py:24
  17.2 0.0 copy-start.2
  17.2 10.1 %all-to-all-start.1 = ((bf16[16,4,64,256]{3,2,1,0:T(8,128)(2,1)}), bf16[16,4,64,256]{3,2,1,0:T(8,128)(2,1)S(1)}, u32[]{:S(2)}, u32[]{:S(2)}) async-start(bf16[16,4,64,256]{3,2,1,0:T(8,128)(2,1)} %broadcast_in_dim.2), calls=%async_computation.2 | async-start | bytes 4194304 | tf_op jit(solution)/shard_map/all_to_all | solution.py:23
  27.4 0.0 copy-done.2
  27.4 0.3 fusion.1
  27.7 1.1 copy.15
  28.8 56.3 %all-to-all-done.1 = bf16[16,4,64,256]{3,2,1,0:T(8,128)(2,1)S(1)} async-done(((bf16[16,4,64,256]{3,2,1,0:T(8,128)(2,1)}), bf16[16,4,64,256]{3,2,1,0:T(8,128)(2,1)S(1)}, u32[]{:S(2)}, u32[]{:S(2)}) %all-to-all-start.1) | async-done | bytes 2097184 | tf_op jit(solution)/shard_map/all_to_all | solution.py:23
  85.1 5.8 %all-to-all-start.3 = ((f32[16,4,16,256]{3,2,1,0:T(8,128)}), f32[16,4,16,256]{3,2,1,0:T(8,128)}, u32[]{:S(2)}, u32[]{:S(2)}) async-start(f32[16,4,16,256]{3,2,1,0:T(8,128)} %bitcast.32), calls=%async_computation.4 | async-start | bytes 2097152 | tf_op jit(solution)/shard_map/all_to_all | solution.py:17
  91.0 0.1 copy.7
  91.1 0.7 convolution_bitcast_fusion.1
  91.9 0.9 copy.9
  92.8 28.8 %all-to-all-done.3 = f32[16,4,16,256]{3,2,1,0:T(8,128)} async-done(((f32[16,4,16,256]{3,2,1,0:T(8,128)}), f32[16,4,16,256]{3,2,1,0:T(8,128)}, u32[]{:S(2)}, u32[]{:S(2)}) %all-to-all-start.3) | async-done | bytes 1048608 | tf_op jit(solution)/shard_map/all_to_all | solution.py:17
  121.6 6.6 %all-to-all-start.2 = ((f32[16,4,1024]{2,1,0:T(4,128)}), f32[16,4,1024]{2,1,0:T(4,128)S(1)}, u32[]{:S(2)}, u32[]{:S(2)}) async-start(f32[16,4,1024]{2,1,0:T(4,128)} %copy.9), calls=%async_computation.3 | async-start | bytes 524288 | tf_op jit(solution)/shard_map/all_to_all | solution.py:17
  128.2 2.2 %reduce-scatter.2.cloned.1.call-done = f32[64,1024]{1,0:T(8,128)} async-done(((f32[1024,1024]{1,0:T(8,128)}), f32[64,1024]{1,0:T(8,128)}) %reduce-scatter.2.cloned.1.call-update) | async-done | bytes 262160 | tf_op jit(solution)/shard_map/reduce_scatter | solution.py:44
  130.3 1.8 %reshape.24 = f32[16,4,1024]{2,1,0:T(4,128)} reshape(f32[64,1024]{1,0:T(8,128)} %reduce-scatter.2.cloned.1.call-done) | data formatting | bytes 524288 | tf_op jit(solution)/shard_map/reshape | solution.py:11
  132.1 4.0 %all-to-all-done.2 = f32[16,4,1024]{2,1,0:T(4,128)S(1)} async-done(((f32[16,4,1024]{2,1,0:T(4,128)}), f32[16,4,1024]{2,1,0:T(4,128)S(1)}, u32[]{:S(2)}, u32[]{:S(2)}) %all-to-all-start.2) | async-done | bytes 262176 | tf_op jit(solution)/shard_map/all_to_all | solution.py:17
  136.1 3.9 %all-to-all-start = ((f32[16,4,1024]{2,1,0:T(4,128)}), f32[16,4,1024]{2,1,0:T(4,128)S(1)}, u32[]{:S(2)}, u32[]{:S(2)}) async-start(f32[16,4,1024]{2,1,0:T(4,128)} %reshape.24), calls=%async_computation.1 | async-start | bytes 524288 | tf_op jit(solution)/shard_map/all_to_all | solution.py:17
  140.0 1.9 %reduce_sum.29 = f32[4,16,256]{2,1,0:T(8,128)} reduce(f32[16,4,16,256]{3,2,1,0:T(8,128)} %all-to-all-done.3, f32[]{:T(128)} %constant.0.clone.1), dimensions={0}, to_apply=%region_3.0 | reduce | flops 245760 | bytes 1114116 | tf_op jit(solution)/shard_map/reduce_sum | solution.py:18
  141.9 0.1 reduce_sum.28
  142.0 0.6 broadcast_multiply_fusion
  142.6 4.9 %all-to-all-done = f32[16,4,1024]{2,1,0:T(4,128)S(1)} async-done(((f32[16,4,1024]{2,1,0:T(4,128)}), f32[16,4,1024]{2,1,0:T(4,128)S(1)}, u32[]{:S(2)}, u32[]{:S(2)}) %all-to-all-start) | async-done | bytes 262176 | tf_op jit(solution)/shard_map/all_to_all | solution.py:17
  147.5 0.1 reduce_sum.27
  147.5 0.6 broadcast_multiply_fusion.1
  (1 shorter events, 0.0 us)
Async XLA Ops:
  7.2 1.2 copy-start
  7.2 123.1 %reduce-scatter.2.cloned.1.call-start = ((), (), s32[]{:S(2)}) async-start(), calls=%async_computation.5 | async-start | bytes 4456448 | tf_op jit(solution)/shard_map/reduce_scatter | solution.py:44
  13.4 1.2 copy-start.1
  17.2 10.1 %copy-start.2 = (bf16[64,256]{1,0:T(8,128)(2,1)S(1)}, bf16[64,256]{1,0:T(8,128)(2,1)}, u32[]{:S(2)}) copy-start(bf16[64,256]{1,0:T(8,128)(2,1)} %param.5) | copy-start | bytes 98308
  17.2 67.9 %all-to-all-start.1 = ((bf16[16,4,64,256]{3,2,1,0:T(8,128)(2,1)}), bf16[16,4,64,256]{3,2,1,0:T(8,128)(2,1)S(1)}, u32[]{:S(2)}, u32[]{:S(2)}) async-start(bf16[16,4,64,256]{3,2,1,0:T(8,128)(2,1)} %broadcast_in_dim.2), calls=%async_computation.2 | async-start | bytes 4194304 | tf_op jit(solution)/shard_map/all_to_all | solution.py:23
  85.1 36.5 %all-to-all-start.3 = ((f32[16,4,16,256]{3,2,1,0:T(8,128)}), f32[16,4,16,256]{3,2,1,0:T(8,128)}, u32[]{:S(2)}, u32[]{:S(2)}) async-start(f32[16,4,16,256]{3,2,1,0:T(8,128)} %bitcast.32), calls=%async_computation.4 | async-start | bytes 2097152 | tf_op jit(solution)/shard_map/all_to_all | solution.py:17
  121.6 14.5 %all-to-all-start.2 = ((f32[16,4,1024]{2,1,0:T(4,128)}), f32[16,4,1024]{2,1,0:T(4,128)S(1)}, u32[]{:S(2)}, u32[]{:S(2)}) async-start(f32[16,4,1024]{2,1,0:T(4,128)} %copy.9), calls=%async_computation.3 | async-start | bytes 524288 | tf_op jit(solution)/shard_map/all_to_all | solution.py:17
  136.1 11.4 %all-to-all-start = ((f32[16,4,1024]{2,1,0:T(4,128)}), f32[16,4,1024]{2,1,0:T(4,128)S(1)}, u32[]{:S(2)}, u32[]{:S(2)}) async-start(f32[16,4,1024]{2,1,0:T(4,128)} %reshape.24), calls=%async_computation.1 | async-start | bytes 524288 | tf_op jit(solution)/shard_map/all_to_all | solution.py:17
Sparse Core Ops, SparseCore 0:
  13.6 116.6 reduce-scatter.1
where the time goes:
time: 156 us; the launch traced here: 155 us
  waiting for transfers between devices  96.2 us (62%)
  starting transfers between devices  26.4 us (17%)
  between operations  14.1 us (9%)
  local copies, waits for them, and re-layouts  7.86 us (5%)
  matrix products  7.11 us (5%)
  other arithmetic  3.26 us (2%)
    all_to_all x1, waiting for transfers between devices, copy_for_each(): lax.all_to_all(jnp.broadcast_to(array[None], (devices, *array.shape)), ax...  56.3 us
    all_to_all x3, waiting for transfers between devices, sum_at_owner(): lax.all_to_all(blocks, axis, split_axis=0, concat_axis=0, tiled=True)  37.7 us
    all_to_all x3, starting transfers between devices, sum_at_owner(): lax.all_to_all(blocks, axis, split_axis=0, concat_axis=0, tiled=True)  16.3 us
    all_to_all x1, starting transfers between devices, copy_for_each(): lax.all_to_all(jnp.broadcast_to(array[None], (devices, *array.shape)), ax...  10.1 us
    dot_general x1, matrix products, shards(): jnp.dot(flat.T, flat, precision=lax.Precision.HIGHEST, preferred_element_...  5.03 us
  transfers between devices with their start and end apart: 5, of which 5 were waited for; matrix products, arithmetic and copies ran while one was open for 7% of the time, Pallas kernels for 0%

commit v1 on v0

v1 whole, which is shorter than its diff:
```python
import math

import jax
import jax.numpy as jnp
from jax import lax
from jax.experimental import pallas as pl
from jax.experimental.pallas import tpu as pltpu
from jax.sharding import PartitionSpec as P

MESH = pl.DeviceIdType.MESH
F32 = jnp.float32
BF16 = jnp.bfloat16


def hi_lo(x):
    hi = x.astype(BF16)
    return hi, (x - hi.astype(F32)).astype(BF16)


def groups_of_four(parts):
    rows, width = parts[0].shape
    n = rows // 8
    first = lax.broadcasted_iota(jnp.int32, (n, 8, width), 1) < 4

    def pair(a, b):
        a, b = a.reshape(n, 8, width), b.reshape(n, 8, width)
        low = jnp.where(first, a, pltpu.roll(b, 4, axis=1))
        high = jnp.where(first, pltpu.roll(a, 4, axis=1), b)
        return low, high

    low_a, high_a = pair(parts[0], parts[1])
    low_b, high_b = pair(parts[2], parts[3])
    return jnp.concatenate([low_a, low_b], axis=1), jnp.concatenate([high_a, high_b], axis=1)


def kernel(
    norms, sizes, tensor, factor_one, factor_two, gram_one, gram_two, reduced,
    x_v, f1_v, f2_v, lhs, rhs, part, to_sib, from_sib, to_plane, from_plane, to_line, from_line,
    core, f2_out, f2_in, g2_out, g2_in,
    load_sem, up_send, up_recv, down_send, down_recv, sib_send, sib_recv, half_send, half_recv,
    plane_send, plane_recv, line_send, line_recv, f2_send, f2_recv, g2_send, g2_recv,
):
    n_ja, n_ka = sizes
    n_z = n_ja // 2
    ja, ka = lax.axis_index("ja"), lax.axis_index("ka")
    z, c = ja // 2, ja % 2
    sib = z * 2 + (1 - c)
    loads = [
        pltpu.make_async_copy(src, dst, load_sem.at[i])
        for i, (src, dst) in enumerate(((tensor, x_v), (factor_one, f1_v), (factor_two, f2_v)))
    ]
    for load in loads:
        load.start()

    barrier = pltpu.get_barrier_semaphore()

    def greet_ja(d, carry):
        pl.semaphore_signal(barrier, inc=1, device_id={"ja": (ja + d) % n_ja}, device_id_type=MESH)
        return carry

    def greet_ka(d, carry):
        pl.semaphore_signal(barrier, inc=1, device_id={"ka": (ka + d) % n_ka}, device_id_type=MESH)
        return carry

    lax.fori_loop(1, n_ja, greet_ja, 0)
    lax.fori_loop(1, n_ka, greet_ka, 0)

    for load in loads:
        load.wait()
    x = x_v[...].reshape(256, 1024)
    x_hi, x_lo = hi_lo(x)
    rhs[0:256] = x_hi
    rhs[256:512] = x_lo
    rhs[512:768] = x_hi
    for block in range(8):
        turned = x[:, block * 128 : (block + 1) * 128].T
        t_hi, t_lo = hi_lo(turned)
        for half in range(2):
            rows = slice(half * 64, (half + 1) * 64)
            lhs[half, block, :, 0:256] = t_hi[rows]
            lhs[half, block, :, 256:512] = t_hi[rows]
            lhs[half, block, :, 512:768] = t_lo[rows]
    f_hi, f_lo = hi_lo(f1_v[...])
    mine = jnp.dot(x_hi, f_hi, preferred_element_type=F32)
    mine += jnp.dot(x_hi, f_lo, preferred_element_type=F32)
    mine += jnp.dot(x_lo, f_hi, preferred_element_type=F32)
    own_row = pl.multiple_of(ja * 64, 64)
    core[:, pl.ds(own_row, 64), :] = mine.astype(BF16).reshape(4, 64, 256)
    f2_out[...] = f2_v[...].astype(F32).T.astype(BF16).reshape(n_ja, 16, 64)
    f2_in[pl.ds(ja, 1)] = f2_out[pl.ds(ja, 1)]

    pl.semaphore_wait(barrier, n_ja + n_ka - 2)

    def block_of(chunk, source_z, source_c):
        row = pl.multiple_of(source_z * 128 + source_c * 64, 64)
        return core.at[pl.ds(chunk * 2, 2), pl.ds(row, 64), :]

    def ring_copy(up, chunk, hop):
        source = (z - (hop - 1) + n_z) % n_z if up else (z + (hop - 1)) % n_z
        target = (z + 1) % n_z if up else (z - 1 + n_z) % n_z
        block = block_of(chunk, source, c)
        send, recv = (up_send, up_recv) if up else (down_send, down_recv)
        return pltpu.make_async_remote_copy(
            block, block, send.at[chunk, hop - 1], recv.at[chunk, hop - 1],
            device_id={"ja": target * 2 + c}, device_id_type=MESH,
        )

    def arrival(up, chunk, hop):
        source = (z - hop + n_z) % n_z if up else (z + hop) % n_z
        block = block_of(chunk, source, c)
        send, recv = (up_send, up_recv) if up else (down_send, down_recv)
        return pltpu.make_async_remote_copy(
            block, block, send.at[chunk, hop - 1], recv.at[chunk, hop - 1],
            device_id={"ja": sib}, device_id_type=MESH,
        )

    def sib_copy(chunk, source_z, slot, source_c):
        block = block_of(chunk, source_z, source_c)
        return pltpu.make_async_remote_copy(
            block, block, sib_send.at[chunk, slot], sib_recv.at[chunk, slot],
            device_id={"ja": sib}, device_id_type=MESH,
        )

    last_hop = {(True, 0): 4, (True, 1): 3, (False, 0): 3, (False, 1): 4}
    for chunk in range(2):
        for up in (True, False):
            ring_copy(up, chunk, 1).start()
    for chunk in range(2):
        sib_copy(chunk, z, 0, c).start()

    def f2_copy(d):
        to = (ja + d) % n_ja
        return pltpu.make_async_remote_copy(
            f2_out.at[to], f2_in.at[ja], f2_send.at[to], f2_recv.at[ja],
            device_id={"ja": to}, device_id_type=MESH,
        )

    def f2_arrival(d):
        source = (ja + d) % n_ja
        return pltpu.make_async_remote_copy(
            f2_out.at[source], f2_in.at[source], f2_send.at[source], f2_recv.at[source],
            device_id={"ja": source}, device_id_type=MESH,
        )

    def start_f2(d, carry):
        f2_copy(d).start()
        return carry

    lax.fori_loop(1, n_ja, start_f2, 0)

    def product(half):
        left = lhs[half].reshape(512, 768)
        for block in range(4):
            columns = slice(block * 256, (block + 1) * 256)
            part[:, :, columns] = jnp.dot(left, rhs[:, columns], preferred_element_type=F32).reshape(8, 64, 256)

    pair = ka // 2

    def rows_of(m):
        at = pl.ds(pl.multiple_of(m * 8, 8), 8)
        low_a, high_a = groups_of_four([part[i, at, :] for i in range(4)])
        low_b, high_b = groups_of_four([part[4 + i, at, :] for i in range(4)])
        return (
            jnp.concatenate([low_a[0], low_b[0]], axis=0),
            jnp.concatenate([high_a[0], high_b[0]], axis=0),
        )

    def half_copy(m):
        return pltpu.make_async_remote_copy(
            to_sib.at[m], from_sib.at[m], half_send.at[m], half_recv.at[m],
            device_id={"ja": sib}, device_id_type=MESH,
        )

    product(1 - c)

    def give(dm, carry):
        m = (pair + dm) % 8
        low, high = rows_of(m)
        to_sib[m, 0] = low.astype(BF16)
        to_sib[m, 1] = high.astype(BF16)
        half_copy(m).start()
        return carry

    lax.fori_loop(1, 9, give, 0)
    product(c)

    def plane_copy(to):
        return pltpu.make_async_remote_copy(
            to_plane.at[to // 2, to % 2], from_plane.at[ka], plane_send.at[to], plane_recv.at[ka],
            device_id={"ka": to}, device_id_type=MESH,
        )

    def plane_arrival(source):
        return pltpu.make_async_remote_copy(
            to_plane.at[source // 2, source % 2], from_plane.at[source], plane_send.at[source],
            plane_recv.at[source], device_id={"ka": source}, device_id_type=MESH,
        )

    def combine(m):
        half_copy(m).wait_recv()
        low, high = rows_of(m)
        to_plane[m, 0] = (low + from_sib[m, 0].astype(F32)).astype(BF16)
        to_plane[m, 1] = (high + from_sib[m, 1].astype(F32)).astype(BF16)

    def give_plane(dm, carry):
        m = (pair + dm) % 8
        combine(m)
        plane_copy(m * 2).start()
        plane_copy(m * 2 + 1).start()
        return carry

    lax.fori_loop(1, 8, give_plane, 0)
    combine(pair)
    plane_copy(pair * 2 + 1 - ka % 2).start()

    for hop in range(1, 5):
        for chunk in range(2):
            for up in (True, False):
                if hop > last_hop[up, chunk]:
                    continue
                arrival(up, chunk, hop).wait_recv()
                if hop < last_hop[up, chunk]:
                    ring_copy(up, chunk, hop + 1).start()
                source = (z - hop + n_z) % n_z if up else (z + hop) % n_z
                sib_copy(chunk, source, hop if up else n_z - hop, c).start()
    for slot in range(8):
        for chunk in range(2):
            sib_copy(chunk, (z - slot + n_z) % n_z, slot, 1 - c).wait_recv()

    own = core[:, pl.ds(own_row, 64), :]
    sums = []
    for block in range(4):
        columns = slice(block * 256, (block + 1) * 256)
        total = jnp.zeros((64, 256), F32)
        for k in range(4):
            total += lax.dot_general(
                own[k], core[k, columns, :], (((1,), (1,)), ((), ())), preferred_element_type=F32
            )
        sums.append(total)
    low, high = groups_of_four(sums)
    g2_out[:, 0] = low.astype(BF16)
    g2_out[:, 1] = high.astype(BF16)

    def g2_copy(to):
        return pltpu.make_async_remote_copy(
            g2_out.at[to // 2, to % 2], g2_in.at[ka], g2_send.at[to], g2_recv.at[ka],
            device_id={"ka": to}, device_id_type=MESH,
        )

    def g2_arrival(source):
        return pltpu.make_async_remote_copy(
            g2_out.at[source // 2, source % 2], g2_in.at[source], g2_send.at[source], g2_recv.at[source],
            device_id={"ka": source}, device_id_type=MESH,
        )

    def start_g2(d, carry):
        g2_copy((ka + d) % n_ka).start()
        return carry

    lax.fori_loop(1, n_ka, start_g2, 0)

    def end_f2(d, carry):
        f2_arrival(d).wait_recv()
        return carry

    lax.fori_loop(1, n_ja, end_f2, 0)
    f2 = jnp.concatenate([f2_in[i].astype(F32) for i in range(n_ja)], axis=1).astype(BF16)
    for k in range(4):
        reduced[k] = jnp.dot(f2, core[k], preferred_element_type=F32)

    def add_plane(d, total):
        source = (ka + d) % n_ka
        plane_arrival(source).wait_recv()
        return total + from_plane[source].astype(F32)

    total = lax.fori_loop(1, n_ka, add_plane, to_plane[pair, ka % 2].astype(F32))
    low, high = groups_of_four([total[:, i * 256 : (i + 1) * 256] for i in range(4)])
    to_line[:, 0] = low.astype(BF16)
    to_line[:, 1] = high.astype(BF16)

    def line_copy(to):
        return pltpu.make_async_remote_copy(
            to_line.at[to // 2, to % 2], from_line.at[z], line_send.at[to], line_recv.at[z],
            device_id={"ja": to * 2 + c}, device_id_type=MESH,
        )

    def line_arrival(source):
        return pltpu.make_async_remote_copy(
            to_line.at[source // 2, source % 2], from_line.at[source], line_send.at[source],
            line_recv.at[source], device_id={"ja": source * 2 + c}, device_id_type=MESH,
        )

    def start_line(d, carry):
        line_copy((z + d) % n_z).start()
        return carry

    lax.fori_loop(1, n_z, start_line, 0)

    def add_g2(d, total):
        source = (ka + d) % n_ka
        g2_arrival(source).wait_recv()
        return total + g2_in[source].astype(F32)

    total = lax.fori_loop(1, n_ka, add_g2, g2_out[pair, ka % 2].astype(F32)) * norms[1]
    for i in range(4):
        gram_two[:, i * 256 : (i + 1) * 256] = total[i * 4 : (i + 1) * 4]

    def add_line(d, total):
        source = (z + d) % n_z
        line_arrival(source).wait_recv()
        return total + from_line[source].astype(F32)

    total = lax.fori_loop(1, n_z, add_line, to_line[z // 2, z % 2].astype(F32)) * norms[0]
    for i in range(4):
        gram_one[:, i * 256 : (i + 1) * 256] = total[i * 4 : (i + 1) * 4]

    for chunk in range(2):
        for up in (True, False):
            for hop in range(1, last_hop[up, chunk] + 1):
                ring_copy(up, chunk, hop).wait_send()
        for slot in range(8):
            sib_copy(chunk, (z - slot + n_z) % n_z, slot, c).wait_send()

    def end_ja(d, carry):
        f2_copy(d).wait_send()
        return carry

    def end_ka(d, carry):
        to = (ka + d) % n_ka
        plane_copy(to).wait_send()
        g2_copy(to).wait_send()
        return carry

    def end_z(d, carry):
        line_copy((z + d) % n_z).wait_send()
        return carry

    def end_half(m, carry):
        half_copy(m).wait_send()
        return carry

    lax.fori_loop(1, n_ja, end_ja, 0)
    lax.fori_loop(1, n_ka, end_ka, 0)
    lax.fori_loop(1, n_z, end_z, 0)
    lax.fori_loop(0, 8, end_half, 0)


def solution(mesh):
    n_ja, n_ka = mesh.shape["ja"], mesh.shape["ka"]

    def shards(tensor, factor_one, factor_two):
        slices, owned, width = tensor.shape
        norm_one = 1.0 / math.sqrt(owned * n_ja * slices * n_ka)
        norm_two = 1.0 / math.sqrt(slices * n_ka * factor_one.shape[1])
        dma = pltpu.SemaphoreType.DMA

        def body(*refs):
            kernel((norm_one, norm_two), (n_ja, n_ka), *refs)

        return pl.pallas_call(
            body,
            out_shape=(
                jax.ShapeDtypeStruct((4, 1024), F32),
                jax.ShapeDtypeStruct((4, 1024), F32),
                jax.ShapeDtypeStruct((4, 16, 256), F32),
            ),
            in_specs=[pl.BlockSpec(memory_space=pl.ANY)] * 3,
            out_specs=[pl.BlockSpec(memory_space=pltpu.VMEM)] * 3,
            scratch_shapes=[
                pltpu.VMEM((4, 64, 1024), F32),
                pltpu.VMEM((1024, 256), F32),
                pltpu.VMEM((64, 256), BF16),
                pltpu.VMEM((2, 8, 64, 768), BF16),
                pltpu.VMEM((768, 1024), BF16),
                pltpu.VMEM((8, 64, 1024), F32),
                pltpu.VMEM((8, 2, 32, 1024), BF16),
                pltpu.VMEM((8, 2, 32, 1024), BF16),
                pltpu.VMEM((8, 2, 32, 1024), BF16),
                pltpu.VMEM((16, 32, 1024), BF16),
                pltpu.VMEM((4, 2, 16, 256), BF16),
                pltpu.VMEM((8, 16, 256), BF16),
                pltpu.VMEM((4, 1024, 256), BF16),
                pltpu.VMEM((16, 16, 64), BF16),
                pltpu.VMEM((16, 16, 64), BF16),
                pltpu.VMEM((8, 2, 16, 256), BF16),
                pltpu.VMEM((16, 16, 256), BF16),
                dma((3,)),
                dma((2, 4)), dma((2, 4)), dma((2, 4)), dma((2, 4)),
                dma((2, 8)), dma((2, 8)),
                dma((8,)), dma((8,)),
                dma((16,)), dma((16,)),
                dma((8,)), dma((8,)),
                dma((16,)), dma((16,)),
                dma((16,)), dma((16,)),
            ],
            compiler_params=pltpu.CompilerParams(
                collective_id=0, has_side_effects=True, vmem_limit_bytes=48 * 1024 * 1024
            ),
        )(tensor, factor_one, factor_two)

    return jax.shard_map(
        shards,
        mesh=mesh,
        in_specs=(P("ka", "ja", None), P(), P("ja", None)),
        out_specs=(P(("ja", "ka"), None), P(("ja", "ka"), None), P("ka", "ja", None)),
        check_vma=False,
    )
```

time: 156 us -> 46.1 us (0.30)
  the two profiles are of different devices: /device:TPU:1 before, /device:TPU:28 now
where the time goes in v1:
time: 46.1 us; the launch traced here: 45.9 us
  Pallas kernels  40.2 us (87%)
  local copies, waits for them, and re-layouts  5.04 us (11%)
  between operations  0.65 us (1%)
    pallas_call x1, Pallas kernels, shards(): pl.pallas_call(body, out_shape=(jax.ShapeDtypeStruct((4, 1024), F32), jax...  40.2 us
    unnamed x9, local copies, waits for them, and re-layouts  5.04 us

profile of v1, /device:TPU:28, one launch (start us, length us, event | category | flops | bytes accessed | tf_op | source)
XLA Modules:
  0.0 45.9 jit_solution(1625146630438861960)
XLA Ops:
  0.6 0.0 copy-start
  0.6 1.2 %copy-done = f32[4,64,1024]{2,1,0:T(8,128)S(1)} copy-done((f32[4,64,1024]{2,1,0:T(8,128)S(1)}, f32[4,64,1024]{2,1,0:T(8,128)}, u32[]{:S(2)}) %copy-start) | copy-done | bytes 1048600
  1.9 0.0 copy-start.1
  1.9 1.2 %copy-done.1 = f32[1024,256]{1,0:T(8,128)S(1)} copy-done((f32[1024,256]{1,0:T(8,128)S(1)}, f32[1024,256]{1,0:T(8,128)}, u32[]{:S(2)}) %copy-start.1) | copy-done | bytes 1048600
  3.1 0.0 copy-start.2
  3.1 0.8 %copy-done.2 = bf16[64,256]{1,0:T(8,128)(2,1)S(1)} copy-done((bf16[64,256]{1,0:T(8,128)(2,1)S(1)}, bf16[64,256]{1,0:T(8,128)(2,1)}, u32[]{:S(2)}) %copy-start.2) | copy-done | bytes 32792
  3.8 40.2 %shard_map.58 = (f32[4,1024]{1,0:T(4,128)S(1)}, f32[4,1024]{1,0:T(4,128)S(1)}, f32[4,16,256]{2,1,0:T(8,128)S(1)}) custom-call(f32[4,64,1024]{2,1,0:T(8,128)S(1)} %copy-done, f32[1024,256]{1,0:T(8,128)S(1)} %copy-done.1, bf16[64,256]{1,0:T(8,128)(2,1)S(1)} %copy-done.2), custom_call_target="tpu_custom_call" | custom-call | tf_op jit(solution)/shard_map/pallas_call | solution.py:360
  44.0 0.6 %copy.9 = f32[4,1024]{1,0:T(4,128)} copy(f32[4,1024]{1,0:T(4,128)S(1)} %get-tuple-element.6) | data formatting | bytes 32768
  44.7 0.6 %copy.10 = f32[4,1024]{1,0:T(4,128)} copy(f32[4,1024]{1,0:T(4,128)S(1)} %get-tuple-element.7) | data formatting | bytes 32768
  45.3 0.6 %copy.11 = f32[4,16,256]{2,1,0:T(8,128)} copy(f32[4,16,256]{2,1,0:T(8,128)S(1)} %get-tuple-element.8) | data formatting | bytes 131072
Async XLA Ops:
  0.6 1.2 %copy-start = (f32[4,64,1024]{2,1,0:T(8,128)S(1)}, f32[4,64,1024]{2,1,0:T(8,128)}, u32[]{:S(2)}) copy-start(f32[4,64,1024]{2,1,0:T(8,128)} %refs_0_.1) | copy-start | bytes 3145732
  1.9 1.2 %copy-start.1 = (f32[1024,256]{1,0:T(8,128)S(1)}, f32[1024,256]{1,0:T(8,128)}, u32[]{:S(2)}) copy-start(f32[1024,256]{1,0:T(8,128)} %refs_1_.1) | copy-start | bytes 3145732
  3.1 0.8 %copy-start.2 = (bf16[64,256]{1,0:T(8,128)(2,1)S(1)}, bf16[64,256]{1,0:T(8,128)(2,1)}, u32[]{:S(2)}) copy-start(bf16[64,256]{1,0:T(8,128)(2,1)} %refs_2_.1) | copy-start | bytes 98308

commit v2 on v1

--- a/solution.py
+++ b/solution.py
@@ -35,10 +35,10 @@
 
 def kernel(
     norms, sizes, tensor, factor_one, factor_two, gram_one, gram_two, reduced,
-    x_v, f1_v, f2_v, lhs, rhs, part, to_sib, from_sib, to_plane, from_plane, to_line, from_line,
-    core, f2_out, f2_in, g2_out, g2_in,
+    x_v, f1_v, f2_v, lhs, rhs, part, to_sib, from_sib, to_plane, far, near, to_cross, far_cross, near_cross,
+    to_line, from_line, core, f2_out, f2_in, g2_out, g2_in, known,
     load_sem, up_send, up_recv, down_send, down_recv, sib_send, sib_recv, half_send, half_recv,
-    plane_send, plane_recv, line_send, line_recv, f2_send, f2_recv, g2_send, g2_recv,
+    plane_send, plane_recv, cross_send, cross_recv, line_send, line_recv, f2_send, f2_recv, g2_send, g2_recv,
 ):
     n_ja, n_ka = sizes
     n_z = n_ja // 2
@@ -54,32 +54,31 @@
 
     barrier = pltpu.get_barrier_semaphore()
 
-    def greet_ja(d, carry):
-        pl.semaphore_signal(barrier, inc=1, device_id={"ja": (ja + d) % n_ja}, device_id_type=MESH)
-        return carry
-
-    def greet_ka(d, carry):
-        pl.semaphore_signal(barrier, inc=1, device_id={"ka": (ka + d) % n_ka}, device_id_type=MESH)
-        return carry
-
-    lax.fori_loop(1, n_ja, greet_ja, 0)
-    lax.fori_loop(1, n_ka, greet_ka, 0)
+    x, y = ka // 4, ka % 4
+    z_next = [((z + step) % n_z) * 2 + c for step in (1, n_z - 1)]
+    x_next = [((x + step) % 4) * 4 + y for step in (1, 3)]
+    y_next = [x * 4 + (y + step) % 4 for step in (1, 3)]
+
+    def tell(semaphore, axis, peers):
+        for peer in peers:
+            pl.semaphore_signal(semaphore, inc=1, device_id={axis: peer}, device_id_type=MESH)
+
+    tell(barrier, "ja", [sib] + z_next)
+    tell(barrier, "ka", x_next + y_next)
+
+    def learn(step):
+        if step > 0:
+            pl.semaphore_wait(known.at[0, step - 1], 2)
+            pl.semaphore_wait(known.at[1, step - 1], 2)
+        if step < 3:
+            tell(known.at[0, step], "ka", x_next if step == 0 else y_next)
+            tell(known.at[1, step], "ja", z_next)
+        else:
+            tell(known.at[1, 3], "ja", [sib])
 
     for load in loads:
         load.wait()
-    x = x_v[...].reshape(256, 1024)
-    x_hi, x_lo = hi_lo(x)
-    rhs[0:256] = x_hi
-    rhs[256:512] = x_lo
-    rhs[512:768] = x_hi
-    for block in range(8):
-        turned = x[:, block * 128 : (block + 1) * 128].T
-        t_hi, t_lo = hi_lo(turned)
-        for half in range(2):
-            rows = slice(half * 64, (half + 1) * 64)
-            lhs[half, block, :, 0:256] = t_hi[rows]
-            lhs[half, block, :, 256:512] = t_hi[rows]
-            lhs[half, block, :, 512:768] = t_lo[rows]
+    x_hi, x_lo = hi_lo(x_v[...].reshape(256, 1024))
     f_hi, f_lo = hi_lo(f1_v[...])
     mine = jnp.dot(x_hi, f_hi, preferred_element_type=F32)
     mine += jnp.dot(x_hi, f_lo, preferred_element_type=F32)
@@ -89,11 +88,11 @@
     f2_out[...] = f2_v[...].astype(F32).T.astype(BF16).reshape(n_ja, 16, 64)
     f2_in[pl.ds(ja, 1)] = f2_out[pl.ds(ja, 1)]
 
-    pl.semaphore_wait(barrier, n_ja + n_ka - 2)
+    pl.semaphore_wait(barrier, 7)
 
     def block_of(chunk, source_z, source_c):
         row = pl.multiple_of(source_z * 128 + source_c * 64, 64)
-        return core.at[pl.ds(chunk * 2, 2), pl.ds(row, 64), :]
+        return core.at[chunk, pl.ds(row, 64), :]
 
     def ring_copy(up, chunk, hop):
         source = (z - (hop - 1) + n_z) % n_z if up else (z + (hop - 1)) % n_z
@@ -121,12 +120,37 @@
             device_id={"ja": sib}, device_id_type=MESH,
         )
 
-    last_hop = {(True, 0): 4, (True, 1): 3, (False, 0): 3, (False, 1): 4}
-    for chunk in range(2):
-        for up in (True, False):
-            ring_copy(up, chunk, 1).start()
-    for chunk in range(2):
+    def last_hop(up, chunk):
+        return 4 if up == (chunk < 2) else 3
+
+    order = [(up, chunk) for pair in zip((0, 1, 2, 3), (2, 3, 0, 1)) for up, chunk in zip((True, False), pair)]
+    for up, chunk in order:
+        ring_copy(up, chunk, 1).start()
+    for chunk in range(4):
         sib_copy(chunk, z, 0, c).start()
+    learn(0)
+
+    def pass_on(hop):
+        for up, chunk in order:
+            if hop > last_hop(up, chunk):
+                continue
+            arrival(up, chunk, hop).wait_recv()
+            if hop < last_hop(up, chunk):
+                ring_copy(up, chunk, hop + 1).start()
+            source = (z - hop + n_z) % n_z if up else (z + hop) % n_z
+            sib_copy(chunk, source, hop if up else n_z - hop, c).start()
+
+    rhs[0:256] = x_hi
+    rhs[256:512] = x_lo
+    rhs[512:768] = x_hi
+    for block in range(8):
+        turned = x_v[:, :, block * 128 : (block + 1) * 128].reshape(256, 128).T
+        t_hi, t_lo = hi_lo(turned)
+        for half in range(2):
+            rows = slice(half * 64, (half + 1) * 64)
+            lhs[half, block, :, 0:256] = t_hi[rows]
+            lhs[half, block, :, 256:512] = t_hi[rows]
+            lhs[half, block, :, 512:768] = t_lo[rows]
 
     def f2_copy(d):
         to = (ja + d) % n_ja
@@ -145,16 +169,12 @@
     def start_f2(d, carry):
         f2_copy(d).start()
         return carry
-
-    lax.fori_loop(1, n_ja, start_f2, 0)
 
     def product(half):
         left = lhs[half].reshape(512, 768)
         for block in range(4):
             columns = slice(block * 256, (block + 1) * 256)
             part[:, :, columns] = jnp.dot(left, rhs[:, columns], preferred_element_type=F32).reshape(8, 64, 256)
-
-    pair = ka // 2
 
     def rows_of(m):
         at = pl.ds(pl.multiple_of(m * 8, 8), 8)
@@ -173,58 +193,107 @@
 
     product(1 - c)
 
-    def give(dm, carry):
-        m = (pair + dm) % 8
-        low, high = rows_of(m)
-        to_sib[m, 0] = low.astype(BF16)
-        to_sib[m, 1] = high.astype(BF16)
-        half_copy(m).start()
-        return carry
-
-    lax.fori_loop(1, 9, give, 0)
+    def give(row):
+        def body(h, carry):
+            m = row * 2 + h
+            low, high = rows_of(m)
+            to_sib[m, 0] = low.astype(BF16)
+            to_sib[m, 1] = high.astype(BF16)
+            half_copy(m).start()
+            return carry
+
+        lax.fori_loop(0, 2, body, 0)
+
+    for step in (2, 1, 3, 0):
+        give((x + step) % 4)
+    learn(1)
+    pass_on(1)
     product(c)
-
-    def plane_copy(to):
-        return pltpu.make_async_remote_copy(
-            to_plane.at[to // 2, to % 2], from_plane.at[ka], plane_send.at[to], plane_recv.at[ka],
-            device_id={"ka": to}, device_id_type=MESH,
-        )
-
-    def plane_arrival(source):
-        return pltpu.make_async_remote_copy(
-            to_plane.at[source // 2, source % 2], from_plane.at[source], plane_send.at[source],
-            plane_recv.at[source], device_id={"ka": source}, device_id_type=MESH,
-        )
-
-    def combine(m):
-        half_copy(m).wait_recv()
-        low, high = rows_of(m)
-        to_plane[m, 0] = (low + from_sib[m, 0].astype(F32)).astype(BF16)
-        to_plane[m, 1] = (high + from_sib[m, 1].astype(F32)).astype(BF16)
-
-    def give_plane(dm, carry):
-        m = (pair + dm) % 8
-        combine(m)
-        plane_copy(m * 2).start()
-        plane_copy(m * 2 + 1).start()
-        return carry
-
-    lax.fori_loop(1, 8, give_plane, 0)
-    combine(pair)
-    plane_copy(pair * 2 + 1 - ka % 2).start()
-
-    for hop in range(1, 5):
-        for chunk in range(2):
-            for up in (True, False):
-                if hop > last_hop[up, chunk]:
-                    continue
-                arrival(up, chunk, hop).wait_recv()
-                if hop < last_hop[up, chunk]:
-                    ring_copy(up, chunk, hop + 1).start()
-                source = (z - hop + n_z) % n_z if up else (z + hop) % n_z
-                sib_copy(chunk, source, hop if up else n_z - hop, c).start()
+    learn(2)
+
+    def half_of(left, half):
+        return slice(left + half * 256, left + (half + 1) * 256)
+
+    def slab(axis, at, lanes):
+        return (pl.ds(at, 1), slice(None), slice(None), lanes) if axis == 0 else (slice(None), pl.ds(at, 1), slice(None), lanes)
+
+    def plane_copy(axis, way, kind):
+        place = x if axis == 0 else y
+        to = (place + (1, 3)[way]) % 4
+        peer = (x_next, y_next)[axis][way]
+        at = (place + 2) % 4 if kind == 0 else to
+        half = 1 - way if kind == 1 else way
+        lanes = half_of(axis * 512, half)
+        source = to_plane.at[at, :, :, lanes] if axis == 0 else to_plane.at[:, at, :, lanes]
+        target = far.at[axis, way] if kind == 0 else near.at[axis, way, :, :, half_of(0, half)]
+        return pltpu.make_async_remote_copy(
+            source, target, plane_send.at[axis, way, kind], plane_recv.at[axis, way, kind],
+            device_id={"ka": peer}, device_id_type=MESH,
+        )
+
+    def cross_copy(axis, way, kind):
+        place = y if axis == 0 else x
+        to = (place + (1, 3)[way]) % 4
+        peer = (y_next, x_next)[axis][way]
+        at = (place + 2) % 4 if kind == 0 else to
+        half = 1 - way if kind == 1 else way
+        target = far_cross.at[axis, way] if kind == 0 else near_cross.at[axis, way, :, half_of(0, half)]
+        return pltpu.make_async_remote_copy(
+            to_cross.at[axis, at, :, half_of(0, half)], target,
+            cross_send.at[axis, way, kind], cross_recv.at[axis, way, kind],
+            device_id={"ka": peer}, device_id_type=MESH,
+        )
+
+    def combine(row):
+        def body(h, carry):
+            m = row * 2 + h
+            half_copy(m).wait_recv()
+            low, high = rows_of(m)
+            to_plane[row, h * 2] = (low + from_sib[m, 0].astype(F32)).astype(BF16)
+            to_plane[row, h * 2 + 1] = (high + from_sib[m, 1].astype(F32)).astype(BF16)
+            return carry
+
+        lax.fori_loop(0, 2, body, 0)
+
+    combine((x + 2) % 4)
+    for way in range(2):
+        plane_copy(0, way, 0).start()
+    combine((x + 1) % 4)
+    plane_copy(0, 0, 1).start()
+    combine((x + 3) % 4)
+    plane_copy(0, 1, 1).start()
+    combine(x)
+    for kind in range(2):
+        for way in range(2):
+            plane_copy(1, way, kind).start()
+    learn(3)
+    pass_on(2)
+
+    pl.semaphore_wait(known.at[1, 3], 1)
+    lax.fori_loop(1, n_ja, start_f2, 0)
+
+    for axis in range(2):
+        place = x if axis == 0 else y
+        for way in range(2):
+            plane_copy(axis, way, 0).wait_recv()
+            where = slab(axis, (place + (1, 3)[way]) % 4, half_of(axis * 512, way))
+            mine = to_plane[where]
+            to_plane[where] = (mine.astype(F32) + far[axis, way].reshape(mine.shape).astype(F32)).astype(BF16)
+            plane_copy(axis, way, 2).start()
+    pass_on(3)
+    for axis in range(2):
+        for way in range(2):
+            for kind in (1, 2):
+                plane_copy(axis, way, kind).wait_recv()
+        mine = to_plane[slab(axis, x if axis == 0 else y, slice(axis * 512, axis * 512 + 512))].reshape(4, 32, 512)
+        to_cross[axis] = (mine.astype(F32) + near[axis, 0].astype(F32) + near[axis, 1].astype(F32)).astype(BF16)
+        for kind in range(2):
+            for way in range(2):
+                cross_copy(axis, way, kind).start()
+    pass_on(4)
+
     for slot in range(8):
-        for chunk in range(2):
+        for chunk in range(4):
             sib_copy(chunk, (z - slot + n_z) % n_z, slot, 1 - c).wait_recv()
 
     own = core[:, pl.ds(own_row, 64), :]
@@ -259,6 +328,14 @@
 
     lax.fori_loop(1, n_ka, start_g2, 0)
 
+    for axis in range(2):
+        place = y if axis == 0 else x
+        for way in range(2):
+            cross_copy(axis, way, 0).wait_recv()
+            where = (axis, (place + (1, 3)[way]) % 4, slice(None), half_of(0, way))
+            to_cross[where] = (to_cross[where].astype(F32) + far_cross[axis, way].astype(F32)).astype(BF16)
+            cross_copy(axis, way, 2).start()
+
     def end_f2(d, carry):
         f2_arrival(d).wait_recv()
         return carry
@@ -268,12 +345,14 @@
     for k in range(4):
         reduced[k] = jnp.dot(f2, core[k], preferred_element_type=F32)
 
-    def add_plane(d, total):
-        source = (ka + d) % n_ka
-        plane_arrival(source).wait_recv()
-        return total + from_plane[source].astype(F32)
-
-    total = lax.fori_loop(1, n_ka, add_plane, to_plane[pair, ka % 2].astype(F32))
+    sides = []
+    for axis in range(2):
+        for way in range(2):
+            for kind in (1, 2):
+                cross_copy(axis, way, kind).wait_recv()
+        mine = to_cross[axis, y if axis == 0 else x]
+        sides.append(mine.astype(F32) + near_cross[axis, 0].astype(F32) + near_cross[axis, 1].astype(F32))
+    total = jnp.concatenate(sides, axis=1)
     low, high = groups_of_four([total[:, i * 256 : (i + 1) * 256] for i in range(4)])
     to_line[:, 0] = low.astype(BF16)
     to_line[:, 1] = high.astype(BF16)
@@ -301,7 +380,7 @@
         g2_arrival(source).wait_recv()
         return total + g2_in[source].astype(F32)
 
-    total = lax.fori_loop(1, n_ka, add_g2, g2_out[pair, ka % 2].astype(F32)) * norms[1]
+    total = lax.fori_loop(1, n_ka, add_g2, g2_out[ka // 2, ka % 2].astype(F32)) * norms[1]
     for i in range(4):
         gram_two[:, i * 256 : (i + 1) * 256] = total[i * 4 : (i + 1) * 4]
 
@@ -314,21 +393,24 @@
     for i in range(4):
         gram_one[:, i * 256 : (i + 1) * 256] = total[i * 4 : (i + 1) * 4]
 
-    for chunk in range(2):
+    for chunk in range(4):
         for up in (True, False):
-            for hop in range(1, last_hop[up, chunk] + 1):
+            for hop in range(1, last_hop(up, chunk) + 1):
                 ring_copy(up, chunk, hop).wait_send()
         for slot in range(8):
             sib_copy(chunk, (z - slot + n_z) % n_z, slot, c).wait_send()
+    for axis in range(2):
+        for way in range(2):
+            for kind in range(3):
+                plane_copy(axis, way, kind).wait_send()
+                cross_copy(axis, way, kind).wait_send()
 
     def end_ja(d, carry):
         f2_copy(d).wait_send()
         return carry
 
     def end_ka(d, carry):
-        to = (ka + d) % n_ka
-        plane_copy(to).wait_send()
-        g2_copy(to).wait_send()
+        g2_copy((ka + d) % n_ka).wait_send()
         return carry
 
     def end_z(d, carry):
@@ -375,8 +457,12 @@
                 pltpu.VMEM((8, 64, 1024), F32),
                 pltpu.VMEM((8, 2, 32, 1024), BF16),
                 pltpu.VMEM((8, 2, 32, 1024), BF16),
-                pltpu.VMEM((8, 2, 32, 1024), BF16),
-                pltpu.VMEM((16, 32, 1024), BF16),
+                pltpu.VMEM((4, 4, 32, 1024), BF16),
+                pltpu.VMEM((2, 2, 4, 32, 256), BF16),
+                pltpu.VMEM((2, 2, 4, 32, 512), BF16),
+                pltpu.VMEM((2, 4, 32, 512), BF16),
+                pltpu.VMEM((2, 2, 32, 256), BF16),
+                pltpu.VMEM((2, 2, 32, 512), BF16),
                 pltpu.VMEM((4, 2, 16, 256), BF16),
                 pltpu.VMEM((8, 16, 256), BF16),
                 pltpu.VMEM((4, 1024, 256), BF16),
@@ -384,11 +470,13 @@
                 pltpu.VMEM((16, 16, 64), BF16),
                 pltpu.VMEM((8, 2, 16, 256), BF16),
                 pltpu.VMEM((16, 16, 256), BF16),
+                pltpu.SemaphoreType.REGULAR((2, 4)),
                 dma((3,)),
-                dma((2, 4)), dma((2, 4)), dma((2, 4)), dma((2, 4)),
-                dma((2, 8)), dma((2, 8)),
+                dma((4, 4)), dma((4, 4)), dma((4, 4)), dma((4, 4)),
+                dma((4, 8)), dma((4, 8)),
                 dma((8,)), dma((8,)),
-                dma((16,)), dma((16,)),
+                dma((2, 2, 3)), dma((2, 2, 3)),
+                dma((2, 2, 3)), dma((2, 2, 3)),
                 dma((8,)), dma((8,)),
                 dma((16,)), dma((16,)),
                 dma((16,)), dma((16,)),

time: 46.1 us -> 44.1 us (0.957)
  the two profiles are of different devices: /device:TPU:28 before, /device:TPU:1 now
where the time goes in v2:
time: 44.1 us; the launch traced here: 43.9 us
  Pallas kernels  38.2 us (87%)
  local copies, waits for them, and re-layouts  5.04 us (11%)
  between operations  0.65 us (1%)
    pallas_call x1, Pallas kernels, shards(): pl.pallas_call(body, out_shape=(jax.ShapeDtypeStruct((4, 1024), F32), jax...  38.2 us
    unnamed x9, local copies, waits for them, and re-layouts  5.04 us

profile of v2, /device:TPU:1, one launch (start us, length us, event | category | flops | bytes accessed | tf_op | source)
XLA Modules:
  0.0 43.9 jit_solution(4451938813037696468)
XLA Ops:
  0.6 0.0 copy-start
  0.6 1.2 %copy-done = f32[4,64,1024]{2,1,0:T(8,128)S(1)} copy-done((f32[4,64,1024]{2,1,0:T(8,128)S(1)}, f32[4,64,1024]{2,1,0:T(8,128)}, u32[]{:S(2)}) %copy-start) | copy-done | bytes 1048600
  1.9 0.0 copy-start.1
  1.9 1.2 %copy-done.1 = f32[1024,256]{1,0:T(8,128)S(1)} copy-done((f32[1024,256]{1,0:T(8,128)S(1)}, f32[1024,256]{1,0:T(8,128)}, u32[]{:S(2)}) %copy-start.1) | copy-done | bytes 1048600
  3.1 0.0 copy-start.2
  3.1 0.8 %copy-done.2 = bf16[64,256]{1,0:T(8,128)(2,1)S(1)} copy-done((bf16[64,256]{1,0:T(8,128)(2,1)S(1)}, bf16[64,256]{1,0:T(8,128)(2,1)}, u32[]{:S(2)}) %copy-start.2) | copy-done | bytes 32792
  3.8 38.2 %shard_map.58 = (f32[4,1024]{1,0:T(4,128)S(1)}, f32[4,1024]{1,0:T(4,128)S(1)}, f32[4,16,256]{2,1,0:T(8,128)S(1)}) custom-call(f32[4,64,1024]{2,1,0:T(8,128)S(1)} %copy-done, f32[1024,256]{1,0:T(8,128)S(1)} %copy-done.1, bf16[64,256]{1,0:T(8,128)(2,1)S(1)} %copy-done.2), custom_call_target="tpu_custom_call" | custom-call | tf_op jit(solution)/shard_map/pallas_call | solution.py:442
  42.0 0.6 %copy.9 = f32[4,1024]{1,0:T(4,128)} copy(f32[4,1024]{1,0:T(4,128)S(1)} %get-tuple-element.6) | data formatting | bytes 32768
  42.6 0.6 %copy.10 = f32[4,1024]{1,0:T(4,128)} copy(f32[4,1024]{1,0:T(4,128)S(1)} %get-tuple-element.7) | data formatting | bytes 32768
  43.3 0.6 %copy.11 = f32[4,16,256]{2,1,0:T(8,128)} copy(f32[4,16,256]{2,1,0:T(8,128)S(1)} %get-tuple-element.8) | data formatting | bytes 131072
Async XLA Ops:
  0.6 1.2 %copy-start = (f32[4,64,1024]{2,1,0:T(8,128)S(1)}, f32[4,64,1024]{2,1,0:T(8,128)}, u32[]{:S(2)}) copy-start(f32[4,64,1024]{2,1,0:T(8,128)} %refs_0_.1) | copy-start | bytes 3145732
  1.9 1.2 %copy-start.1 = (f32[1024,256]{1,0:T(8,128)S(1)}, f32[1024,256]{1,0:T(8,128)}, u32[]{:S(2)}) copy-start(f32[1024,256]{1,0:T(8,128)} %refs_1_.1) | copy-start | bytes 3145732
  3.1 0.8 %copy-start.2 = (bf16[64,256]{1,0:T(8,128)(2,1)S(1)}, bf16[64,256]{1,0:T(8,128)(2,1)}, u32[]{:S(2)}) copy-start(bf16[64,256]{1,0:T(8,128)(2,1)} %refs_2_.1) | copy-start | bytes 98308

commit v3 on v2

--- a/solution.py
+++ b/solution.py
@@ -36,7 +36,7 @@
 def kernel(
     norms, sizes, tensor, factor_one, factor_two, gram_one, gram_two, reduced,
     x_v, f1_v, f2_v, lhs, rhs, part, to_sib, from_sib, to_plane, far, near, to_cross, far_cross, near_cross,
-    to_line, from_line, core, f2_out, f2_in, g2_out, g2_in, known,
+    to_line, from_line, core, f2_out, f2_in, g2_out, g2_in,
     load_sem, up_send, up_recv, down_send, down_recv, sib_send, sib_recv, half_send, half_recv,
     plane_send, plane_recv, cross_send, cross_recv, line_send, line_recv, f2_send, f2_recv, g2_send, g2_recv,
 ):
@@ -55,26 +55,19 @@
     barrier = pltpu.get_barrier_semaphore()
 
     x, y = ka // 4, ka % 4
-    z_next = [((z + step) % n_z) * 2 + c for step in (1, n_z - 1)]
     x_next = [((x + step) % 4) * 4 + y for step in (1, 3)]
     y_next = [x * 4 + (y + step) % 4 for step in (1, 3)]
 
-    def tell(semaphore, axis, peers):
-        for peer in peers:
-            pl.semaphore_signal(semaphore, inc=1, device_id={axis: peer}, device_id_type=MESH)
-
-    tell(barrier, "ja", [sib] + z_next)
-    tell(barrier, "ka", x_next + y_next)
-
-    def learn(step):
-        if step > 0:
-            pl.semaphore_wait(known.at[0, step - 1], 2)
-            pl.semaphore_wait(known.at[1, step - 1], 2)
-        if step < 3:
-            tell(known.at[0, step], "ka", x_next if step == 0 else y_next)
-            tell(known.at[1, step], "ja", z_next)
-        else:
-            tell(known.at[1, 3], "ja", [sib])
+    def greet_ja(d, carry):
+        pl.semaphore_signal(barrier, inc=1, device_id={"ja": (ja + d) % n_ja}, device_id_type=MESH)
+        return carry
+
+    def greet_ka(d, carry):
+        pl.semaphore_signal(barrier, inc=1, device_id={"ka": (ka + d) % n_ka}, device_id_type=MESH)
+        return carry
+
+    lax.fori_loop(1, n_ja, greet_ja, 0)
+    lax.fori_loop(1, n_ka, greet_ka, 0)
 
     for load in loads:
         load.wait()
@@ -88,58 +81,6 @@
     f2_out[...] = f2_v[...].astype(F32).T.astype(BF16).reshape(n_ja, 16, 64)
     f2_in[pl.ds(ja, 1)] = f2_out[pl.ds(ja, 1)]
 
-    pl.semaphore_wait(barrier, 7)
-
-    def block_of(chunk, source_z, source_c):
-        row = pl.multiple_of(source_z * 128 + source_c * 64, 64)
-        return core.at[chunk, pl.ds(row, 64), :]
-
-    def ring_copy(up, chunk, hop):
-        source = (z - (hop - 1) + n_z) % n_z if up else (z + (hop - 1)) % n_z
-        target = (z + 1) % n_z if up else (z - 1 + n_z) % n_z
-        block = block_of(chunk, source, c)
-        send, recv = (up_send, up_recv) if up else (down_send, down_recv)
-        return pltpu.make_async_remote_copy(
-            block, block, send.at[chunk, hop - 1], recv.at[chunk, hop - 1],
-            device_id={"ja": target * 2 + c}, device_id_type=MESH,
-        )
-
-    def arrival(up, chunk, hop):
-        source = (z - hop + n_z) % n_z if up else (z + hop) % n_z
-        block = block_of(chunk, source, c)
-        send, recv = (up_send, up_recv) if up else (down_send, down_recv)
-        return pltpu.make_async_remote_copy(
-            block, block, send.at[chunk, hop - 1], recv.at[chunk, hop - 1],
-            device_id={"ja": sib}, device_id_type=MESH,
-        )
-
-    def sib_copy(chunk, source_z, slot, source_c):
-        block = block_of(chunk, source_z, source_c)
-        return pltpu.make_async_remote_copy(
-            block, block, sib_send.at[chunk, slot], sib_recv.at[chunk, slot],
-            device_id={"ja": sib}, device_id_type=MESH,
-        )
-
-    def last_hop(up, chunk):
-        return 4 if up == (chunk < 2) else 3
-
-    order = [(up, chunk) for pair in zip((0, 1, 2, 3), (2, 3, 0, 1)) for up, chunk in zip((True, False), pair)]
-    for up, chunk in order:
-        ring_copy(up, chunk, 1).start()
-    for chunk in range(4):
-        sib_copy(chunk, z, 0, c).start()
-    learn(0)
-
-    def pass_on(hop):
-        for up, chunk in order:
-            if hop > last_hop(up, chunk):
-                continue
-            arrival(up, chunk, hop).wait_recv()
-            if hop < last_hop(up, chunk):
-                ring_copy(up, chunk, hop + 1).start()
-            source = (z - hop + n_z) % n_z if up else (z + hop) % n_z
-            sib_copy(chunk, source, hop if up else n_z - hop, c).start()
-
     rhs[0:256] = x_hi
     rhs[256:512] = x_lo
     rhs[512:768] = x_hi
@@ -152,24 +93,6 @@
             lhs[half, block, :, 256:512] = t_hi[rows]
             lhs[half, block, :, 512:768] = t_lo[rows]
 
-    def f2_copy(d):
-        to = (ja + d) % n_ja
-        return pltpu.make_async_remote_copy(
-            f2_out.at[to], f2_in.at[ja], f2_send.at[to], f2_recv.at[ja],
-            device_id={"ja": to}, device_id_type=MESH,
-        )
-
-    def f2_arrival(d):
-        source = (ja + d) % n_ja
-        return pltpu.make_async_remote_copy(
-            f2_out.at[source], f2_in.at[source], f2_send.at[source], f2_recv.at[source],
-            device_id={"ja": source}, device_id_type=MESH,
-        )
-
-    def start_f2(d, carry):
-        f2_copy(d).start()
-        return carry
-
     def product(half):
         left = lhs[half].reshape(512, 768)
         for block in range(4):
@@ -199,18 +122,89 @@
             low, high = rows_of(m)
             to_sib[m, 0] = low.astype(BF16)
             to_sib[m, 1] = high.astype(BF16)
-            half_copy(m).start()
             return carry
 
         lax.fori_loop(0, 2, body, 0)
 
     for step in (2, 1, 3, 0):
         give((x + step) % 4)
-    learn(1)
-    pass_on(1)
     product(c)
-    learn(2)
-
+
+    pl.semaphore_wait(barrier, n_ja + n_ka - 2)
+
+    def block_of(chunk, source_z, source_c):
+        row = pl.multiple_of(source_z * 128 + source_c * 64, 64)
+        return core.at[chunk, pl.ds(row, 64), :]
+
+    def ring_copy(up, chunk, hop):
+        source = (z - (hop - 1) + n_z) % n_z if up else (z + (hop - 1)) % n_z
+        target = (z + 1) % n_z if up else (z - 1 + n_z) % n_z
+        block = block_of(chunk, source, c)
+        send, recv = (up_send, up_recv) if up else (down_send, down_recv)
+        return pltpu.make_async_remote_copy(
+            block, block, send.at[chunk, hop - 1], recv.at[chunk, hop - 1],
+            device_id={"ja": target * 2 + c}, device_id_type=MESH,
+        )
+
+    def arrival(up, chunk, hop):
+        source = (z - hop + n_z) % n_z if up else (z + hop) % n_z
+        block = block_of(chunk, source, c)
+        send, recv = (up_send, up_recv) if up else (down_send, down_recv)
+        return pltpu.make_async_remote_copy(
+            block, block, send.at[chunk, hop - 1], recv.at[chunk, hop - 1],
+            device_id={"ja": sib}, device_id_type=MESH,
+        )
+
+    def sib_copy(chunk, source_z, slot, source_c):
+        block = block_of(chunk, source_z, source_c)
+        return pltpu.make_async_remote_copy(
+            block, block, sib_send.at[chunk, slot], sib_recv.at[chunk, slot],
+            device_id={"ja": sib}, device_id_type=MESH,
+        )
+
+    def last_hop(up, chunk):
+        return 4 if up == (chunk < 2) else 3
+
+    order = [(up, chunk) for pair in zip((0, 1, 2, 3), (2, 3, 0, 1)) for up, chunk in zip((True, False), pair)]
+    for up, chunk in order:
+        ring_copy(up, chunk, 1).start()
+
+    def pass_on(hop):
+        for up, chunk in order:
+            if hop > last_hop(up, chunk):
+                continue
+            arrival(up, chunk, hop).wait_recv()
+            if hop < last_hop(up, chunk):
+                ring_copy(up, chunk, hop + 1).start()
+            source = (z - hop + n_z) % n_z if up else (z + hop) % n_z
+            sib_copy(chunk, source, hop if up else n_z - hop, c).start()
+
+    def f2_copy(d):
+        to = (ja + d) % n_ja
+        return pltpu.make_async_remote_copy(
+            f2_out.at[to], f2_in.at[ja], f2_send.at[to], f2_recv.at[ja],
+            device_id={"ja": to}, device_id_type=MESH,
+        )
+
+    def f2_arrival(d):
+        source = (ja + d) % n_ja
+        return pltpu.make_async_remote_copy(
+            f2_out.at[source], f2_in.at[source], f2_send.at[source], f2_recv.at[source],
+            device_id={"ja": source}, device_id_type=MESH,
+        )
+
+    def start_f2(d, carry):
+        f2_copy(d).start()
+        return carry
+
+    def start_half(h, carry):
+        half_copy((x * 2 + 4 + h) % 8).start()
+        return carry
+
+    lax.fori_loop(0, 8, start_half, 0)
+    lax.fori_loop(1, n_ja, start_f2, 0)
+    for chunk in range(4):
+        sib_copy(chunk, z, 0, c).start()
     def half_of(left, half):
         return slice(left + half * 256, left + (half + 1) * 256)
 
@@ -266,11 +260,7 @@
     for kind in range(2):
         for way in range(2):
             plane_copy(1, way, kind).start()
-    learn(3)
-    pass_on(2)
-
-    pl.semaphore_wait(known.at[1, 3], 1)
-    lax.fori_loop(1, n_ja, start_f2, 0)
+    pass_on(1)
 
     for axis in range(2):
         place = x if axis == 0 else y
@@ -280,7 +270,7 @@
             mine = to_plane[where]
             to_plane[where] = (mine.astype(F32) + far[axis, way].reshape(mine.shape).astype(F32)).astype(BF16)
             plane_copy(axis, way, 2).start()
-    pass_on(3)
+    pass_on(2)
     for axis in range(2):
         for way in range(2):
             for kind in (1, 2):
@@ -290,6 +280,7 @@
         for kind in range(2):
             for way in range(2):
                 cross_copy(axis, way, kind).start()
+    pass_on(3)
     pass_on(4)
 
     for slot in range(8):
@@ -470,7 +461,6 @@
                 pltpu.VMEM((16, 16, 64), BF16),
                 pltpu.VMEM((8, 2, 16, 256), BF16),
                 pltpu.VMEM((16, 16, 256), BF16),
-                pltpu.SemaphoreType.REGULAR((2, 4)),
                 dma((3,)),
                 dma((4, 4)), dma((4, 4)), dma((4, 4)), dma((4, 4)),
                 dma((4, 8)), dma((4, 8)),

time: 44.1 us -> 44.3 us (level)
  no operation moved by 1% of the time
where the time goes in v3:
time: 44.3 us; the launch traced here: 44.1 us
  Pallas kernels  38.4 us (87%)
  local copies, waits for them, and re-layouts  5.04 us (11%)
  between operations  0.65 us (1%)
    pallas_call x1, Pallas kernels, shards(): pl.pallas_call(body, out_shape=(jax.ShapeDtypeStruct((4, 1024), F32), jax...  38.4 us
    unnamed x9, local copies, waits for them, and re-layouts  5.04 us

profile of v3, /device:TPU:1, one launch (start us, length us, event | category | flops | bytes accessed | tf_op | source)
XLA Modules:
  0.0 44.1 jit_solution(4972296788218305219)
XLA Ops:
  0.6 0.0 copy-start
  0.6 1.2 %copy-done = f32[4,64,1024]{2,1,0:T(8,128)S(1)} copy-done((f32[4,64,1024]{2,1,0:T(8,128)S(1)}, f32[4,64,1024]{2,1,0:T(8,128)}, u32[]{:S(2)}) %copy-start) | copy-done | bytes 1048600
  1.9 0.0 copy-start.1
  1.9 1.2 %copy-done.1 = f32[1024,256]{1,0:T(8,128)S(1)} copy-done((f32[1024,256]{1,0:T(8,128)S(1)}, f32[1024,256]{1,0:T(8,128)}, u32[]{:S(2)}) %copy-start.1) | copy-done | bytes 1048600
  3.1 0.0 copy-start.2
  3.1 0.8 %copy-done.2 = bf16[64,256]{1,0:T(8,128)(2,1)S(1)} copy-done((bf16[64,256]{1,0:T(8,128)(2,1)S(1)}, bf16[64,256]{1,0:T(8,128)(2,1)}, u32[]{:S(2)}) %copy-start.2) | copy-done | bytes 32792
  3.8 38.4 %shard_map.58 = (f32[4,1024]{1,0:T(4,128)S(1)}, f32[4,1024]{1,0:T(4,128)S(1)}, f32[4,16,256]{2,1,0:T(8,128)S(1)}) custom-call(f32[4,64,1024]{2,1,0:T(8,128)S(1)} %copy-done, f32[1024,256]{1,0:T(8,128)S(1)} %copy-done.1, bf16[64,256]{1,0:T(8,128)(2,1)S(1)} %copy-done.2), custom_call_target="tpu_custom_call" | custom-call | tf_op jit(solution)/shard_map/pallas_call | solution.py:433
  42.2 0.6 %copy.9 = f32[4,1024]{1,0:T(4,128)} copy(f32[4,1024]{1,0:T(4,128)S(1)} %get-tuple-element.6) | data formatting | bytes 32768
  42.8 0.6 %copy.10 = f32[4,1024]{1,0:T(4,128)} copy(f32[4,1024]{1,0:T(4,128)S(1)} %get-tuple-element.7) | data formatting | bytes 32768
  43.5 0.6 %copy.11 = f32[4,16,256]{2,1,0:T(8,128)} copy(f32[4,16,256]{2,1,0:T(8,128)S(1)} %get-tuple-element.8) | data formatting | bytes 131072
Async XLA Ops:
  0.6 1.2 %copy-start = (f32[4,64,1024]{2,1,0:T(8,128)S(1)}, f32[4,64,1024]{2,1,0:T(8,128)}, u32[]{:S(2)}) copy-start(f32[4,64,1024]{2,1,0:T(8,128)} %refs_0_.1) | copy-start | bytes 3145732
  1.9 1.2 %copy-start.1 = (f32[1024,256]{1,0:T(8,128)S(1)}, f32[1024,256]{1,0:T(8,128)}, u32[]{:S(2)}) copy-start(f32[1024,256]{1,0:T(8,128)} %refs_1_.1) | copy-start | bytes 3145732
  3.1 0.8 %copy-start.2 = (bf16[64,256]{1,0:T(8,128)(2,1)S(1)}, bf16[64,256]{1,0:T(8,128)(2,1)}, u32[]{:S(2)}) copy-start(bf16[64,256]{1,0:T(8,128)(2,1)} %refs_2_.1) | copy-start | bytes 98308

commit v4 on v3

--- a/solution.py
+++ b/solution.py
@@ -283,9 +283,47 @@
     pass_on(3)
     pass_on(4)
 
+    for axis in range(2):
+        place = y if axis == 0 else x
+        for way in range(2):
+            cross_copy(axis, way, 0).wait_recv()
+            where = (axis, (place + (1, 3)[way]) % 4, slice(None), half_of(0, way))
+            to_cross[where] = (to_cross[where].astype(F32) + far_cross[axis, way].astype(F32)).astype(BF16)
+            cross_copy(axis, way, 2).start()
+
     for slot in range(8):
         for chunk in range(4):
             sib_copy(chunk, (z - slot + n_z) % n_z, slot, 1 - c).wait_recv()
+
+    sides = []
+    for axis in range(2):
+        for way in range(2):
+            for kind in (1, 2):
+                cross_copy(axis, way, kind).wait_recv()
+        mine = to_cross[axis, y if axis == 0 else x]
+        sides.append(mine.astype(F32) + near_cross[axis, 0].astype(F32) + near_cross[axis, 1].astype(F32))
+    total = jnp.concatenate(sides, axis=1)
+    low, high = groups_of_four([total[:, i * 256 : (i + 1) * 256] for i in range(4)])
+    to_line[:, 0] = low.astype(BF16)
+    to_line[:, 1] = high.astype(BF16)
+
+    def line_copy(to):
+        return pltpu.make_async_remote_copy(
+            to_line.at[to // 2, to % 2], from_line.at[z], line_send.at[to], line_recv.at[z],
+            device_id={"ja": to * 2 + c}, device_id_type=MESH,
+        )
+
+    def line_arrival(source):
+        return pltpu.make_async_remote_copy(
+            to_line.at[source // 2, source % 2], from_line.at[source], line_send.at[source],
+            line_recv.at[source], device_id={"ja": source * 2 + c}, device_id_type=MESH,
+        )
+
+    def start_line(d, carry):
+        line_copy((z + d) % n_z).start()
+        return carry
+
+    lax.fori_loop(1, n_z, start_line, 0)
 
     own = core[:, pl.ds(own_row, 64), :]
     sums = []
@@ -319,14 +357,6 @@
 
     lax.fori_loop(1, n_ka, start_g2, 0)
 
-    for axis in range(2):
-        place = y if axis == 0 else x
-        for way in range(2):
-            cross_copy(axis, way, 0).wait_recv()
-            where = (axis, (place + (1, 3)[way]) % 4, slice(None), half_of(0, way))
-            to_cross[where] = (to_cross[where].astype(F32) + far_cross[axis, way].astype(F32)).astype(BF16)
-            cross_copy(axis, way, 2).start()
-
     def end_f2(d, carry):
         f2_arrival(d).wait_recv()
         return carry
@@ -335,36 +365,6 @@
     f2 = jnp.concatenate([f2_in[i].astype(F32) for i in range(n_ja)], axis=1).astype(BF16)
     for k in range(4):
         reduced[k] = jnp.dot(f2, core[k], preferred_element_type=F32)
-
-    sides = []
-    for axis in range(2):
-        for way in range(2):
-            for kind in (1, 2):
-                cross_copy(axis, way, kind).wait_recv()
-        mine = to_cross[axis, y if axis == 0 else x]
-        sides.append(mine.astype(F32) + near_cross[axis, 0].astype(F32) + near_cross[axis, 1].astype(F32))
-    total = jnp.concatenate(sides, axis=1)
-    low, high = groups_of_four([total[:, i * 256 : (i + 1) * 256] for i in range(4)])
-    to_line[:, 0] = low.astype(BF16)
-    to_line[:, 1] = high.astype(BF16)
-
-    def line_copy(to):
-        return pltpu.make_async_remote_copy(
-            to_line.at[to // 2, to % 2], from_line.at[z], line_send.at[to], line_recv.at[z],
-            device_id={"ja": to * 2 + c}, device_id_type=MESH,
-        )
-
-    def line_arrival(source):
-        return pltpu.make_async_remote_copy(
-            to_line.at[source // 2, source % 2], from_line.at[source], line_send.at[source],
-            line_recv.at[source], device_id={"ja": source * 2 + c}, device_id_type=MESH,
-        )
-
-    def start_line(d, carry):
-        line_copy((z + d) % n_z).start()
-        return carry
-
-    lax.fori_loop(1, n_z, start_line, 0)
 
     def add_g2(d, total):
         source = (ka + d) % n_ka

time: 44.3 us -> 42.6 us (0.962)
  the two profiles are of different devices: /device:TPU:1 before, /device:TPU:8 now
where the time goes in v4:
time: 42.6 us; the launch traced here: 42.4 us
  Pallas kernels  36.7 us (86%)
  local copies, waits for them, and re-layouts  5.04 us (12%)
  between operations  0.65 us (2%)
    pallas_call x1, Pallas kernels, shards(): pl.pallas_call(body, out_shape=(jax.ShapeDtypeStruct((4, 1024), F32), jax...  36.7 us
    unnamed x9, local copies, waits for them, and re-layouts  5.04 us

profile of v4, /device:TPU:8, one launch (start us, length us, event | category | flops | bytes accessed | tf_op | source)
XLA Modules:
  0.0 42.4 jit_solution(17882671681478181498)
XLA Ops:
  0.6 0.0 copy-start
  0.6 1.2 %copy-done = f32[4,64,1024]{2,1,0:T(8,128)S(1)} copy-done((f32[4,64,1024]{2,1,0:T(8,128)S(1)}, f32[4,64,1024]{2,1,0:T(8,128)}, u32[]{:S(2)}) %copy-start) | copy-done | bytes 1048600
  1.9 0.0 copy-start.1
  1.9 1.2 %copy-done.1 = f32[1024,256]{1,0:T(8,128)S(1)} copy-done((f32[1024,256]{1,0:T(8,128)S(1)}, f32[1024,256]{1,0:T(8,128)}, u32[]{:S(2)}) %copy-start.1) | copy-done | bytes 1048600
  3.1 0.0 copy-start.2
  3.1 0.8 %copy-done.2 = bf16[64,256]{1,0:T(8,128)(2,1)S(1)} copy-done((bf16[64,256]{1,0:T(8,128)(2,1)S(1)}, bf16[64,256]{1,0:T(8,128)(2,1)}, u32[]{:S(2)}) %copy-start.2) | copy-done | bytes 32792
  3.8 36.7 %shard_map.58 = (f32[4,1024]{1,0:T(4,128)S(1)}, f32[4,1024]{1,0:T(4,128)S(1)}, f32[4,16,256]{2,1,0:T(8,128)S(1)}) custom-call(f32[4,64,1024]{2,1,0:T(8,128)S(1)} %copy-done, f32[1024,256]{1,0:T(8,128)S(1)} %copy-done.1, bf16[64,256]{1,0:T(8,128)(2,1)S(1)} %copy-done.2), custom_call_target="tpu_custom_call" | custom-call | tf_op jit(solution)/shard_map/pallas_call | solution.py:433
  40.6 0.6 %copy.9 = f32[4,1024]{1,0:T(4,128)} copy(f32[4,1024]{1,0:T(4,128)S(1)} %get-tuple-element.6) | data formatting | bytes 32768
  41.2 0.6 %copy.10 = f32[4,1024]{1,0:T(4,128)} copy(f32[4,1024]{1,0:T(4,128)S(1)} %get-tuple-element.7) | data formatting | bytes 32768
  41.8 0.6 %copy.11 = f32[4,16,256]{2,1,0:T(8,128)} copy(f32[4,16,256]{2,1,0:T(8,128)S(1)} %get-tuple-element.8) | data formatting | bytes 131072
Async XLA Ops:
  0.6 1.2 %copy-start = (f32[4,64,1024]{2,1,0:T(8,128)S(1)}, f32[4,64,1024]{2,1,0:T(8,128)}, u32[]{:S(2)}) copy-start(f32[4,64,1024]{2,1,0:T(8,128)} %refs_0_.1) | copy-start | bytes 3145732
  1.9 1.2 %copy-start.1 = (f32[1024,256]{1,0:T(8,128)S(1)}, f32[1024,256]{1,0:T(8,128)}, u32[]{:S(2)}) copy-start(f32[1024,256]{1,0:T(8,128)} %refs_1_.1) | copy-start | bytes 3145732
  3.1 0.8 %copy-start.2 = (bf16[64,256]{1,0:T(8,128)(2,1)S(1)}, bf16[64,256]{1,0:T(8,128)(2,1)}, u32[]{:S(2)}) copy-start(bf16[64,256]{1,0:T(8,128)(2,1)} %refs_2_.1) | copy-start | bytes 98308

commit v5 on v3

--- a/solution.py
+++ b/solution.py
@@ -283,6 +283,14 @@
     pass_on(3)
     pass_on(4)
 
+    for axis in range(2):
+        place = y if axis == 0 else x
+        for way in range(2):
+            cross_copy(axis, way, 0).wait_recv()
+            where = (axis, (place + (1, 3)[way]) % 4, slice(None), half_of(0, way))
+            to_cross[where] = (to_cross[where].astype(F32) + far_cross[axis, way].astype(F32)).astype(BF16)
+            cross_copy(axis, way, 2).start()
+
     for slot in range(8):
         for chunk in range(4):
             sib_copy(chunk, (z - slot + n_z) % n_z, slot, 1 - c).wait_recv()
@@ -319,23 +327,6 @@
 
     lax.fori_loop(1, n_ka, start_g2, 0)
 
-    for axis in range(2):
-        place = y if axis == 0 else x
-        for way in range(2):
-            cross_copy(axis, way, 0).wait_recv()
-            where = (axis, (place + (1, 3)[way]) % 4, slice(None), half_of(0, way))
-            to_cross[where] = (to_cross[where].astype(F32) + far_cross[axis, way].astype(F32)).astype(BF16)
-            cross_copy(axis, way, 2).start()
-
-    def end_f2(d, carry):
-        f2_arrival(d).wait_recv()
-        return carry
-
-    lax.fori_loop(1, n_ja, end_f2, 0)
-    f2 = jnp.concatenate([f2_in[i].astype(F32) for i in range(n_ja)], axis=1).astype(BF16)
-    for k in range(4):
-        reduced[k] = jnp.dot(f2, core[k], preferred_element_type=F32)
-
     sides = []
     for axis in range(2):
         for way in range(2):
@@ -365,6 +356,15 @@
         return carry
 
     lax.fori_loop(1, n_z, start_line, 0)
+
+    def end_f2(d, carry):
+        f2_arrival(d).wait_recv()
+        return carry
+
+    lax.fori_loop(1, n_ja, end_f2, 0)
+    f2 = jnp.concatenate([f2_in[i].astype(F32) for i in range(n_ja)], axis=1).astype(BF16)
+    for k in range(4):
+        reduced[k] = jnp.dot(f2, core[k], preferred_element_type=F32)
 
     def add_g2(d, total):
         source = (ka + d) % n_ka

time: 44.3 us -> 41.9 us (0.946)
  Pallas kernels: 38.4 us -> 36 us
    pallas_call x1, Pallas kernels: 38.4 us -> 36 us  [shards(): pl.pallas_call(body, out_shape=(jax.ShapeDtypeStruct((4, 1024), F32), jax...]
where the time goes in v5:
time: 41.9 us; the launch traced here: 41.6 us
  Pallas kernels  36 us (86%)
  local copies, waits for them, and re-layouts  5.04 us (12%)
  between operations  0.65 us (2%)
    pallas_call x1, Pallas kernels, shards(): pl.pallas_call(body, out_shape=(jax.ShapeDtypeStruct((4, 1024), F32), jax...  36 us
    unnamed x9, local copies, waits for them, and re-layouts  5.04 us

profile of v5, /device:TPU:1, one launch (start us, length us, event | category | flops | bytes accessed | tf_op | source)
XLA Modules:
  0.0 41.6 jit_solution(3220923912283053688)
XLA Ops:
  0.6 0.0 copy-start
  0.6 1.2 %copy-done = f32[4,64,1024]{2,1,0:T(8,128)S(1)} copy-done((f32[4,64,1024]{2,1,0:T(8,128)S(1)}, f32[4,64,1024]{2,1,0:T(8,128)}, u32[]{:S(2)}) %copy-start) | copy-done | bytes 1048600
  1.9 0.0 copy-start.1
  1.9 1.2 %copy-done.1 = f32[1024,256]{1,0:T(8,128)S(1)} copy-done((f32[1024,256]{1,0:T(8,128)S(1)}, f32[1024,256]{1,0:T(8,128)}, u32[]{:S(2)}) %copy-start.1) | copy-done | bytes 1048600
  3.1 0.0 copy-start.2
  3.1 0.8 %copy-done.2 = bf16[64,256]{1,0:T(8,128)(2,1)S(1)} copy-done((bf16[64,256]{1,0:T(8,128)(2,1)S(1)}, bf16[64,256]{1,0:T(8,128)(2,1)}, u32[]{:S(2)}) %copy-start.2) | copy-done | bytes 32792
  3.8 36.0 %shard_map.58 = (f32[4,1024]{1,0:T(4,128)S(1)}, f32[4,1024]{1,0:T(4,128)S(1)}, f32[4,16,256]{2,1,0:T(8,128)S(1)}) custom-call(f32[4,64,1024]{2,1,0:T(8,128)S(1)} %copy-done, f32[1024,256]{1,0:T(8,128)S(1)} %copy-done.1, bf16[64,256]{1,0:T(8,128)(2,1)S(1)} %copy-done.2), custom_call_target="tpu_custom_call" | custom-call | tf_op jit(solution)/shard_map/pallas_call | solution.py:433
  39.8 0.6 %copy.9 = f32[4,1024]{1,0:T(4,128)} copy(f32[4,1024]{1,0:T(4,128)S(1)} %get-tuple-element.6) | data formatting | bytes 32768
  40.4 0.6 %copy.10 = f32[4,1024]{1,0:T(4,128)} copy(f32[4,1024]{1,0:T(4,128)S(1)} %get-tuple-element.7) | data formatting | bytes 32768
  41.0 0.6 %copy.11 = f32[4,16,256]{2,1,0:T(8,128)} copy(f32[4,16,256]{2,1,0:T(8,128)S(1)} %get-tuple-element.8) | data formatting | bytes 131072
Async XLA Ops:
  0.6 1.2 %copy-start = (f32[4,64,1024]{2,1,0:T(8,128)S(1)}, f32[4,64,1024]{2,1,0:T(8,128)}, u32[]{:S(2)}) copy-start(f32[4,64,1024]{2,1,0:T(8,128)} %refs_0_.1) | copy-start | bytes 3145732
  1.9 1.2 %copy-start.1 = (f32[1024,256]{1,0:T(8,128)S(1)}, f32[1024,256]{1,0:T(8,128)}, u32[]{:S(2)}) copy-start(f32[1024,256]{1,0:T(8,128)} %refs_1_.1) | copy-start | bytes 3145732
  3.1 0.8 %copy-start.2 = (bf16[64,256]{1,0:T(8,128)(2,1)S(1)}, bf16[64,256]{1,0:T(8,128)(2,1)}, u32[]{:S(2)}) copy-start(bf16[64,256]{1,0:T(8,128)(2,1)} %refs_2_.1) | copy-start | bytes 98308
